TPU v7x, 32 devices: a whole 2x2x4 slice. The times are simulated.
32 devices in a mesh: child: 4 (over y, x), shard: 8 (over z, core).
Axes of the slice: x: 2, y: 2, z: 4, core: 2. Of those that a mesh axis runs over, the one named last changes fastest.
Arguments:
- child_tensors: bfloat16 [4, 256, 256, 256], P('child', 'shard'), may hold values from -6 to 6
- leg_ops: bfloat16 [8, 256, 256], replicated, may hold values from -0.375 to 0.375
- term_ops: int32 [4, 4, 2], P('child'), may hold values from 0 to 7
- term_coef: float32 [4, 4], P('child'), may hold values from 0.5 to 1.5
- parent: bfloat16 [4, 256, 256], P('child', 'shard'), may hold values from -0.375 to 0.375
- top_env: float32 [256, 256], replicated, may hold values from -6 to 6
Outputs:
- applied: bfloat16 [4, 256, 256, 256], P('child', None, 'shard')
Inputs may be any that keep to these rules, and one draw needn't show every extreme that they name: `term_ops`: each entry names one of the 8 leg operators.
All inputs are finite; a program needn't handle non-finite values.
Results may differ from a plain program's by a relative error of at most 0.0091.
Values may be sent and summed in bfloat16 or wider, within the bound.
A program may use at most 128 MiB of HBM per device.

v0:
```python
import math

import jax
import jax.numpy as jnp
from jax import lax
from jax.sharding import PartitionSpec as P


def shards(child_tensors, leg_ops, term_ops, term_coef, parent, top_env):
    high = lax.Precision.HIGHEST
    tensor = child_tensors[0]
    bond = tensor.shape[1]
    picks = term_ops[0]
    weights = term_coef[0]
    number = weights.shape[0]
    onehot = (picks[:, :, None] == jnp.arange(leg_ops.shape[0])[None, None, :]).astype(jnp.bfloat16)
    chosen = jnp.einsum(
        "tjn,nab->tjab", onehot, leg_ops, preferred_element_type=jnp.float32
    ).astype(jnp.bfloat16)
    left_ops = chosen[:, 0]
    right_ops = chosen[:, 1]
    parent_block = parent[0]
    parent_full = lax.all_gather(parent_block, "shard", axis=0, tiled=True).astype(jnp.float32)
    regrouped = lax.all_to_all(tensor, "shard", split_axis=1, concat_axis=0, tiled=True)
    upward = lax.all_to_all(tensor, "shard", split_axis=2, concat_axis=0, tiled=True)
    summed = jnp.zeros((bond, bond, upward.shape[2]), jnp.float32)
    for term in range(number):
        image = jnp.einsum(
            "lru,rs->lsu", upward, right_ops[term], preferred_element_type=jnp.float32
        ).astype(jnp.bfloat16)
        summed = summed + weights[term] * jnp.einsum(
            "lk,lsu->ksu", left_ops[term], image, preferred_element_type=jnp.float32
        )
    local = lax.all_to_all(summed, "shard", split_axis=1, concat_axis=2, tiled=True)
    rounded = local.astype(jnp.bfloat16)
    env_part = (
        jnp.einsum("lsu,lsv->uv", regrouped, rounded, preferred_element_type=jnp.float32) / bond
    )
    block_rows = parent_block.astype(jnp.float32)
    env = lax.psum(env_part, "shard")
    lifted = jnp.dot(parent_full.T, jnp.dot(env, parent_full, precision=high), precision=high)
    total = lax.psum(lifted, "child")
    coupling = total - lifted + top_env
    factor = 1.0 / math.sqrt(bond * lax.axis_size("child"))
    partial_hole = (
        jnp.dot(jnp.dot(block_rows, coupling, precision=high), parent_full.T, precision=high)
        * factor
    )
    hole = lax.all_gather(partial_hole.astype(jnp.bfloat16), "shard", axis=0, tiled=True)
    result = local + jnp.einsum("lsu,uv->lsv", regrouped, hole, preferred_element_type=jnp.float32)
    return result.astype(jnp.bfloat16)[None]


def solution(mesh):
    in_specs = (
        P("child", "shard", None, None),
        P(),
        P("child", None, None),
        P("child", None),
        P("child", "shard", None),
        P(),
    )
    out_specs = P("child", None, "shard", None)
    return jax.shard_map(shards, mesh=mesh, in_specs=in_specs, out_specs=out_specs, check_vma=False)
```

profile of v0, /device:TPU:0, one launch (start us, length us, event | category | flops | bytes accessed | tf_op | source)
XLA Modules:
  0.0 548.4 jit_solution(6958713158814415964)
XLA Ops:
  6.5 8.0 %copy.56 = bf16[1,32,256,256]{2,1,3,0:T(8,128)(2,1)} copy(bf16[1,32,256,256]{3,2,1,0:T(8,128)(2,1)} %param.6) | data formatting | bytes 8388608 | tf_op args[0]
  14.5 6.4 %all-to-all-start = ((bf16[32,256,256]{1,0,2:T(8,128)(2,1)}), bf16[32,256,256]{1,0,2:T(8,128)(2,1)}, u32[]{:S(2)}, u32[]{:S(2)}) async-start(bf16[32,256,256]{1,0,2:T(8,128)(2,1)} %bitcast.131), calls=%async_computation | async-start | bytes 8388608 | tf_op jit(solution)/shard_map/all_to_all | solution.py:25
  20.9 6.6 %copy.78 = bf16[32,256,256]{2,0,1:T(8,128)(2,1)} copy(bf16[32,256,256]{2,1,0:T(8,128)(2,1)} %bitcast.130) | data formatting | bytes 8388608 | tf_op jit(solution)/shard_map/squeeze | solution.py:11
  27.4 87.5 %all-to-all-done = bf16[32,256,256]{1,0,2:T(8,128)(2,1)} async-done(((bf16[32,256,256]{1,0,2:T(8,128)(2,1)}), bf16[32,256,256]{1,0,2:T(8,128)(2,1)}, u32[]{:S(2)}, u32[]{:S(2)}) %all-to-all-start) | async-done | bytes 4194336 | tf_op jit(solution)/shard_map/all_to_all | solution.py:25
  114.9 4.6 all-to-all-start.2
  119.6 0.9 convolution_convert_fusion
  120.4 0.0 copy-start.5
  120.4 1.7 fusion.61
  122.2 0.1 copy.101
  122.3 0.1 copy.102
  122.5 0.1 copy.100
  122.6 0.1 copy.99
  122.8 0.1 copy.96
  122.9 0.1 copy.97
  123.1 0.1 copy.103
  123.2 0.1 copy.104
  123.4 0.7 fusion.62
  124.0 6.7 %copy.58 = bf16[8,32,256,32]{2,3,1,0:T(8,128)(2,1)} copy(bf16[8,32,256,32]{2,1,3,0:T(8,128)(2,1)} %bitcast.12) | data formatting | bytes 8388608 | tf_op jit(solution)/shard_map/all_to_all | solution.py:25
  130.7 9.6 %fusion.3 = f32[256,256,32]{1,0,2:T(8,128)} fusion(bf16[256,256,32]{1,2,0:T(8,128)(2,1)} %bitcast.126, bf16[1,1,256,256]{2,3,1,0:T(8,128)(2,1)S(1)} %copy.102, bf16[1,1,256,256]{2,3,1,0:T(8,128)(2,1)S(1)} %copy.101), kind=kOutput, calls=%fused_computation.5 | convolution fusion | flops 2149580800 | bytes 12845056 | tf_op jit(solution)/shard_map/lk,lsu->ksu/dot_general | solution.py:31
  140.3 9.6 %fusion.5 = f32[256,256,32]{1,0,2:T(8,128)} fusion(bf16[256,256,32]{1,2,0:T(8,128)(2,1)} %bitcast.127, bf16[1,1,256,256]{2,3,1,0:T(8,128)(2,1)S(1)} %copy.100, bf16[1,1,256,256]{2,3,1,0:T(8,128)(2,1)S(1)} %copy.99), kind=kOutput, calls=%fused_computation.7 | convolution fusion | flops 2149580800 | bytes 12845056 | tf_op jit(solution)/shard_map/lk,lsu->ksu/dot_general | solution.py:31
  149.9 9.9 %fusion.7 = f32[256,256,32]{1,0,2:T(8,128)} fusion(bf16[256,256,32]{1,2,0:T(8,128)(2,1)} %bitcast.128, bf16[1,1,256,256]{2,3,1,0:T(8,128)(2,1)S(1)} %copy.97, bf16[1,1,256,256]{2,3,1,0:T(8,128)(2,1)S(1)} %copy.96), kind=kOutput, calls=%fused_computation.9 | convolution fusion | flops 2149580800 | bytes 12845056 | tf_op jit(solution)/shard_map/lk,lsu->ksu/dot_general | solution.py:31
  159.8 19.6 %multiply_add_fusion = f32[256,256,32]{1,0,2:T(8,128)} fusion(f32[256,256,32]{1,0,2:T(8,128)} %fusion.3, f32[256,256,32]{1,0,2:T(8,128)} %fusion.5, f32[256,256,32]{1,0,2:T(8,128)} %fusion.7, f32[]{:T(128)} %bitcast.27, f32[]{:T(128)} %bitcast.21, f32[]{:T(128)} %bitcast.15, f32[]{:T(128)} %bitcast, bf16[256,256,32]{1,2,0:T(8,128)(2,1)} %bitcast.129, ...), kind=kOutput, calls=%fused_computation.2 | convolution fusion | flops 2164260864 | bytes 38010896 | tf_op jit(solution)/shard_map/lk,lsu->ksu/dot_general | solution.py:31
  179.4 10.3 %copy.75 = f32[256,256,32]{0,2,1:T(8,128)} copy(f32[256,256,32]{1,0,2:T(8,128)} %multiply_add_fusion) | data formatting | bytes 16777216 | tf_op jit(solution)/shard_map/add | solution.py:31
  189.7 23.8 %all-to-all-done.2 = bf16[32,256,256]{2,0,1:T(8,128)(2,1)} async-done(((bf16[32,256,256]{2,0,1:T(8,128)(2,1)}), bf16[32,256,256]{2,0,1:T(8,128)(2,1)}, u32[]{:S(2)}, u32[]{:S(2)}) %all-to-all-start.2) | async-done | bytes 4194336 | tf_op jit(solution)/shard_map/all_to_all | solution.py:24
  213.5 5.0 all-to-all-start.1
  218.5 0.0 all-reduce.3.cloned.1.call-start
  218.5 4.8 copy.80
  223.4 179.0 %all-to-all-done.1 = f32[256,256,32]{0,2,1:T(8,128)} async-done(((f32[256,256,32]{0,2,1:T(8,128)}), f32[256,256,32]{0,2,1:T(8,128)}, u32[]{:S(2)}, u32[]{:S(2)}) %all-to-all-start.1) | async-done | bytes 8388640 | tf_op jit(solution)/shard_map/all_to_all | solution.py:34
  402.3 4.0 convert_element_type.51
  406.4 0.0 copy-start
  406.4 0.5 copy.77
  406.9 1.7 copy-done
  408.6 2.0 fusion.33
  410.5 0.0 all-reduce.3.cloned.1.call-update
  410.6 0.0 all-reduce.5.cloned.1.call-start
  410.6 14.4 %all-gather = bf16[1,256,256]{2,1,0:T(8,128)(2,1)S(1)} all-gather(bf16[1,32,256]{2,1,0:T(8,128)(2,1)S(1)} %copy-done.4), channel_id=2, replica_groups=mesh['child'=4,'shard'=8] {'shard'}, dimensions={1}, use_global_device_ids=true | all-gather | bytes 147456 | tf_op jit(solution)/shard_map/all_gather | solution.py:23
  425.0 40.1 %all-reduce.3.cloned.1.call-done = f32[256,256]{0,1:T(8,128)} async-done(((f32[256,256]{0,1:T(8,128)}), f32[256,256]{0,1:T(8,128)}) %all-reduce.3.cloned.1.call-update) | async-done | bytes 262160 | tf_op jit(solution)/shard_map/psum | solution.py:40
  465.1 1.3 fusion.55
  466.4 1.1 convolution_bitcast_fusion
  467.5 0.0 all-reduce.5.cloned.1.call-update
  467.6 0.1 copy.81
  467.7 8.3 %copy.76 = f32[256,32,8,32]{0,3,2,1:T(8,128)} copy(f32[256,32,8,32]{0,3,1,2:T(8,128)} %bitcast.34) | data formatting | bytes 16777216 | tf_op jit(solution)/shard_map/all_to_all | solution.py:34
  476.0 34.1 %all-reduce.5.cloned.1.call-done = f32[256,256]{0,1:T(8,128)} async-done(((f32[256,256]{0,1:T(8,128)}), f32[256,256]{0,1:T(8,128)}) %all-reduce.5.cloned.1.call-update) | async-done | bytes 262160 | tf_op jit(solution)/shard_map/psum | solution.py:42
  510.1 1.2 fusion.37
  511.4 0.3 fusion.34
  511.6 14.1 %all_gather.7 = bf16[256,256]{1,0:T(8,128)(2,1)S(1)} all-gather(bf16[32,256]{1,0:T(8,128)(2,1)S(1)} %fusion.34), channel_id=1, replica_groups=mesh['child'=4,'shard'=8] {'shard'}, dimensions={0}, use_global_device_ids=true | all-gather | bytes 147456 | tf_op jit(solution)/shard_map/all_gather | solution.py:49
  525.7 8.0 %fusion.31 = bf16[1,256,32,256]{1,3,2,0:T(8,128)(2,1)} fusion(bf16[256,32,256]{2,0,1:T(8,128)(2,1)} %bitcast.132, f32[256,32,8,32]{0,3,2,1:T(8,128)} %copy.76, bf16[256,256]{1,0:T(8,128)(2,1)S(1)} %all_gather.7), kind=kOutput, calls=%fused_computation.23 | convolution fusion | flops 1077936128 | bytes 16908288 | tf_op jit(solution)/shard_map/lsu,uv->lsv/dot_general | solution.py:50
  533.7 7.8 %copy.82 = bf16[1,256,32,256]{3,2,1,0:T(8,128)(2,1)} copy(bf16[1,256,32,256]{1,3,2,0:T(8,128)(2,1)} %fusion.31) | data formatting | bytes 8388608 | tf_op jit(solution)/shard_map/broadcast_in_dim | solution.py:51
  (11 shorter events, 0.0 us)
Async XLA Ops:
  14.5 100.4 %all-to-all-start = ((bf16[32,256,256]{1,0,2:T(8,128)(2,1)}), bf16[32,256,256]{1,0,2:T(8,128)(2,1)}, u32[]{:S(2)}, u32[]{:S(2)}) async-start(bf16[32,256,256]{1,0,2:T(8,128)(2,1)} %bitcast.131), calls=%async_computation | async-start | bytes 8388608 | tf_op jit(solution)/shard_map/all_to_all | solution.py:25
  27.4 92.1 %copy-start.2 = (bf16[8,256,256]{2,1,0:T(8,128)(2,1)S(1)}, bf16[8,256,256]{2,1,0:T(8,128)(2,1)}, u32[]{:S(2)}) copy-start(bf16[8,256,256]{2,1,0:T(8,128)(2,1)} %param.7) | copy-start | bytes 3145732
  27.4 92.1 %copy-start.6 = (s32[1,4,2]{1,2,0:T(2,128)S(1)}, s32[1,4,2]{1,2,0:T(2,128)}, u32[]{:S(2)}) copy-start(s32[1,4,2]{1,2,0:T(2,128)} %param.8) | copy-start | bytes 100
  114.9 98.6 %all-to-all-start.2 = ((bf16[32,256,256]{2,0,1:T(8,128)(2,1)}), bf16[32,256,256]{2,0,1:T(8,128)(2,1)}, u32[]{:S(2)}, u32[]{:S(2)}) async-start(bf16[32,256,256]{2,0,1:T(8,128)(2,1)} %copy.78), calls=%async_computation.2 | async-start | bytes 8388608 | tf_op jit(solution)/shard_map/all_to_all | solution.py:24
  120.4 2.9 copy-start.5
  213.5 188.8 %all-to-all-start.1 = ((f32[256,256,32]{0,2,1:T(8,128)}), f32[256,256,32]{0,2,1:T(8,128)}, u32[]{:S(2)}, u32[]{:S(2)}) async-start(f32[256,256,32]{0,2,1:T(8,128)} %copy.75), calls=%async_computation.1 | async-start | bytes 16777216 | tf_op jit(solution)/shard_map/all_to_all | solution.py:34
  218.5 246.6 %all-reduce.3.cloned.1.call-start = ((), (), s32[]{:S(2)}) async-start(), calls=%async_computation.3 | async-start | bytes 524288 | tf_op jit(solution)/shard_map/psum | solution.py:40
  406.4 2.2 copy-start
  408.6 2.1 copy-start.4
  408.6 59.0 %copy-start.3 = (f32[256,256]{1,0:T(8,128)S(1)}, f32[256,256]{1,0:T(8,128)}, u32[]{:S(2)}) copy-start(f32[256,256]{1,0:T(8,128)} %param.11) | copy-start | bytes 786436
  410.6 99.6 %all-reduce.5.cloned.1.call-start = ((), (), s32[]{:S(2)}) async-start(), calls=%async_computation.4 | async-start | bytes 524288 | tf_op jit(solution)/shard_map/psum | solution.py:42
  467.7 42.4 %copy-start.1 = (f32[256,256]{0,1:T(8,128)S(1)}, f32[256,256]{0,1:T(8,128)}, u32[]{:S(2)}) copy-start(f32[256,256]{0,1:T(8,128)} %convolution_bitcast_fusion) | copy-start | bytes 786436
Sparse Core Ops, SparseCore 0:
  410.7 54.3 all-reduce.2
  468.0 42.0 all-reduce.4
where the time goes:
time: 550 us; the launch traced here: 548 us
  waiting for transfers between devices  365 us (66%)
  matrix products  63.5 us (12%)
  local copies, waits for them, and re-layouts  58.4 us (11%)
  blocking collectives  28.4 us (5%)
  starting transfers between devices  16 us (3%)
  between operations  13.6 us (2%)
    all_to_all x1, waiting for transfers between devices, shards(): lax.all_to_all(summed, 'shard', split_axis=1, concat_axis=2, tiled=True)  179 us
    all_to_all x1, waiting for transfers between devices, shards(): lax.all_to_all(tensor, 'shard', split_axis=2, concat_axis=0, tiled=True)  87.5 us
    dot_general x4, matrix products, shards(): jnp.einsum('lk,lsu->ksu', left_ops[term], image, preferred_element_type=j...  48.7 us
    psum x1, waiting for transfers between devices, shards(): env = lax.psum(env_part, 'shard')  40.1 us
    psum x1, waiting for transfers between devices, shards(): total = lax.psum(lifted, 'child')  34.1 us
    all_to_all x1, waiting for transfers between devices, shards(): lax.all_to_all(tensor, 'shard', split_axis=1, concat_axis=0, tiled=True)  23.8 us
    all_gather x1, blocking collectives, shards(): lax.all_gather(parent_block, 'shard', axis=0, tiled=True)  14.4 us
    all_gather x1, blocking collectives, shards(): lax.all_gather(partial_hole.astype(jnp.bfloat16), 'shard', axis=0, tiled=...  14.1 us
  transfers between devices with their start and end apart: 5, of which 5 were waited for; matrix products, arithmetic and copies ran while one was open for 16% of the time, Pallas kernels for 0%

commit v1 on v0

v1 whole, which is shorter than its diff:
```python
import functools
import math

import jax
import jax.numpy as jnp
from jax import lax
from jax.experimental import pallas as pl
from jax.experimental.pallas import tpu as pltpu
from jax.sharding import PartitionSpec as P

MESH = pl.DeviceIdType.MESH
HIGH = lax.Precision.HIGHEST


def tail_kernel(
    n, nc, bond, factor, env_ref, par_ref, top_ref, hole_ref,
    parv, envv, envf, lif, chv, cpf, ssem, rsem,
):
    me = lax.axis_index("shard")
    kid = lax.axis_index("child")
    rows, width = env_ref.shape[1], env_ref.shape[2]
    peers = [lax.rem(me + k, n) for k in range(1, n)]
    kids = [lax.rem(kid + k, nc) for k in range(1, nc)]
    barrier = pltpu.get_barrier_semaphore()
    for j in peers:
        pl.semaphore_signal(barrier, inc=1, device_id={"shard": j}, device_id_type=MESH)
    for j in kids:
        pl.semaphore_signal(barrier, inc=1, device_id={"child": j}, device_id_type=MESH)
    pl.semaphore_wait(barrier, n + nc - 2)

    def send(phase, src, dst, axis, j, own):
        copy = pltpu.make_async_remote_copy(
            src_ref=src, dst_ref=dst, send_sem=ssem.at[phase, j], recv_sem=rsem.at[phase, own],
            device_id={axis: j}, device_id_type=MESH,
        )
        copy.start()
        return copy

    def arrive(phase, ref, axis, j):
        pltpu.make_async_remote_copy(
            src_ref=ref, dst_ref=ref, send_sem=ssem.at[phase, j], recv_sem=rsem.at[phase, j],
            device_id={axis: j}, device_id_type=MESH,
        ).wait_recv()

    sent = [send(0, env_ref.at[j], envv.at[me], "shard", j, me) for j in peers]
    sent += [send(1, par_ref, parv.at[me], "shard", j, me) for j in peers]
    parv[me] = par_ref[...]
    total = env_ref[me]
    for j in peers:
        arrive(0, envv.at[j], "shard", j)
        total = total + envv[j]
    envf[me] = total
    sent += [send(2, envf.at[me], envf.at[me], "shard", j, me) for j in peers]
    for j in peers:
        arrive(1, parv.at[j], "shard", j)
    lift = parv[...].astype(jnp.float32).reshape(n * rows, width)
    for j in peers:
        arrive(2, envf.at[j], "shard", j)
    env = envf[...].reshape(n * rows, width) * (1.0 / bond)
    half = jnp.dot(env, lift, precision=HIGH, preferred_element_type=jnp.float32)
    lifted = lax.dot_general(
        lift, half, (((0,), (0,)), ((), ())), precision=HIGH, preferred_element_type=jnp.float32
    )
    lif[...] = lifted.reshape(n, rows, width)
    sent += [send(3, lif.at[me], chv.at[kid], "child", j, kid) for j in kids]
    slab = top_ref[me]
    for j in kids:
        arrive(3, chv.at[j], "child", j)
        slab = slab + chv[j]
    cpf[me] = slab
    sent += [send(4, cpf.at[me], cpf.at[me], "shard", j, me) for j in peers]
    for j in peers:
        arrive(4, cpf.at[j], "shard", j)
    coupling = cpf[...].reshape(n * rows, width)
    half = jnp.dot(lift, coupling, precision=HIGH, preferred_element_type=jnp.float32)
    hole = lax.dot_general(
        half, lift, (((1,), (1,)), ((), ())), precision=HIGH, preferred_element_type=jnp.float32
    )
    hole_ref[...] = (hole * factor).astype(jnp.bfloat16)
    for copy in sent:
        copy.wait_send()


def hole_of(env_part, parent_block, top_env):
    n, nc = lax.axis_size("shard"), lax.axis_size("child")
    rows, width = parent_block.shape
    bond = env_part.shape[0]
    factor = 1.0 / math.sqrt(bond * nc)
    most = max(n, nc)
    vmem = pl.BlockSpec(memory_space=pltpu.VMEM)
    block = lambda count, kind: pltpu.VMEM((count, rows, width), kind)
    return pl.pallas_call(
        functools.partial(tail_kernel, n, nc, bond, factor),
        out_shape=jax.ShapeDtypeStruct((bond, bond), jnp.bfloat16),
        in_specs=[vmem] * 3,
        out_specs=vmem,
        scratch_shapes=[
            block(n, jnp.bfloat16),
            block(n, jnp.float32),
            block(n, jnp.float32),
            block(n, jnp.float32),
            block(nc, jnp.float32),
            block(n, jnp.float32),
            pltpu.SemaphoreType.DMA((5, most)),
            pltpu.SemaphoreType.DMA((5, most)),
        ],
        compiler_params=pltpu.CompilerParams(collective_id=0, has_side_effects=True),
    )(env_part.reshape(n, rows, bond), parent_block, top_env.reshape(n, rows, width))


def shards(child_tensors, leg_ops, term_ops, term_coef, parent, top_env):
    tensor = child_tensors[0]
    bond = tensor.shape[1]
    picks = term_ops[0]
    weights = term_coef[0]
    number = weights.shape[0]
    left_ops = leg_ops[picks[:, 0]]
    right_ops = leg_ops[picks[:, 1]]
    upward = lax.all_to_all(tensor, "shard", split_axis=2, concat_axis=0, tiled=True)
    regrouped = lax.all_to_all(tensor, "shard", split_axis=1, concat_axis=0, tiled=True)
    summed = jnp.zeros((bond, bond, upward.shape[2]), jnp.float32)
    for term in range(number):
        image = jnp.einsum(
            "lru,rs->lsu", upward, right_ops[term], preferred_element_type=jnp.float32
        ).astype(jnp.bfloat16)
        summed = summed + weights[term] * jnp.einsum(
            "lk,lsu->ksu", left_ops[term], image, preferred_element_type=jnp.float32
        )
    local = lax.all_to_all(
        summed.astype(jnp.bfloat16), "shard", split_axis=1, concat_axis=2, tiled=True
    )
    env_part = jnp.einsum("lsu,lsv->uv", regrouped, local, preferred_element_type=jnp.float32)
    hole = hole_of(env_part, parent[0], top_env)
    result = local.astype(jnp.float32) + jnp.einsum(
        "lsu,uv->lsv", regrouped, hole, preferred_element_type=jnp.float32
    )
    return result.astype(jnp.bfloat16)[None]


def solution(mesh):
    in_specs = (
        P("child", "shard", None, None),
        P(),
        P("child", None, None),
        P("child", None),
        P("child", "shard", None),
        P(),
    )
    out_specs = P("child", None, "shard", None)
    return jax.shard_map(shards, mesh=mesh, in_specs=in_specs, out_specs=out_specs, check_vma=False)
```

time: 550 us -> 364 us (0.66)
  waiting for transfers between devices: 365 us -> 206 us
  Pallas kernels: 0 us -> 31.1 us
  blocking collectives: 28.4 us -> 0 us
  between operations: 13.6 us -> 0.12 us
  local copies, waits for them, and re-layouts: 58.4 us -> 48.7 us
    all_to_all x1, waiting for transfers between devices: 179 us -> 87.3 us  [shards(): lax.all_to_all(summed.astype(jnp.bfloat16), 'shard', split_axis=1, concat...]
    psum x2 -> x0, waiting for transfers between devices: 74.2 us -> none  [the longest x1 40.1 us: shards(): env = lax.psum(env_part, 'shard')]
    pallas_call x0 -> x1, Pallas kernels: none -> 31.1 us  [hole_of(): pl.pallas_call(functools.partial(tail_kernel, n, nc, bond, factor), out_s...]
    all_gather x2 -> x0, blocking collectives: 28.4 us -> none  [the longest x1 14.4 us: shards(): lax.all_gather(parent_block, 'shard', axis=0, tiled=True)]
    add x1 -> x0, local copies, waits for them, and re-layouts: 10.3 us -> none  [shards(): summed + weights[term] * jnp.einsum('lk,lsu->ksu', left_ops[term], image,...]
    all_to_all x1, waiting for transfers between devices: 23.8 us -> 31.4 us  [shards(): lax.all_to_all(tensor, 'shard', split_axis=1, concat_axis=0, tiled=True)]
    convert_element_type x1, local copies, waits for them, and re-layouts: 0.48 us -> 7.83 us  [shards(): summed.astype(jnp.bfloat16)]
  transfers between devices with their start and end apart: 5 -> 3, of which waited for: 5 -> 3; matrix products, arithmetic and copies ran while one was open for 16% -> 21% of each run, Pallas kernels for 0% -> 0%
where the time goes in v1:
time: 364 us; the launch traced here: 363 us
  waiting for transfers between devices  206 us (57%)
  matrix products  61 us (17%)
  local copies, waits for them, and re-layouts  48.7 us (13%)
  Pallas kernels  31.1 us (9%)
  starting transfers between devices  15.7 us (4%)
    all_to_all x1, waiting for transfers between devices, shards(): lax.all_to_all(tensor, 'shard', split_axis=2, concat_axis=0, tiled=True)  87.6 us
    all_to_all x1, waiting for transfers between devices, shards(): lax.all_to_all(summed.astype(jnp.bfloat16), 'shard', split_axis=1, concat...  87.3 us
    dot_general x4, matrix products, shards(): jnp.einsum('lk,lsu->ksu', left_ops[term], image, preferred_element_type=j...  45.9 us
    all_to_all x1, waiting for transfers between devices, shards(): lax.all_to_all(tensor, 'shard', split_axis=1, concat_axis=0, tiled=True)  31.4 us
    pallas_call x1, Pallas kernels, hole_of(): pl.pallas_call(functools.partial(tail_kernel, n, nc, bond, factor), out_s...  31.1 us
    dot_general x1, matrix products, shards(): jnp.einsum('lsu,uv->lsv', regrouped, hole, preferred_element_type=jnp.flo...  8.82 us
    unnamed x13, local copies, waits for them, and re-layouts  8.53 us
    convert_element_type x1, local copies, waits for them, and re-layouts, shards(): summed.astype(jnp.bfloat16)  7.83 us
  transfers between devices with their start and end apart: 3, of which 3 were waited for; matrix products, arithmetic and copies ran while one was open for 21% of the time, Pallas kernels for 0%

profile of v1, /device:TPU:0, one launch (start us, length us, event | category | flops | bytes accessed | tf_op | source)
XLA Modules:
  0.0 362.9 jit_solution(8685430397918456353)
XLA Ops:
  0.0 0.0 copy-start
  0.0 7.9 %copy.79 = bf16[1,32,256,256]{2,1,3,0:T(8,128)(2,1)} copy(bf16[1,32,256,256]{3,2,1,0:T(8,128)(2,1)} %param.6) | data formatting | bytes 8388608 | tf_op args[0]
  7.9 6.4 %all-to-all-start = ((bf16[32,256,256]{1,0,2:T(8,128)(2,1)}), bf16[32,256,256]{1,0,2:T(8,128)(2,1)}, u32[]{:S(2)}, u32[]{:S(2)}) async-start(bf16[32,256,256]{1,0,2:T(8,128)(2,1)} %bitcast.109), calls=%async_computation | async-start | bytes 8388608 | tf_op jit(solution)/shard_map/all_to_all | solution.py:119
  14.3 6.5 %copy.98 = bf16[32,256,256]{2,0,1:T(8,128)(2,1)} copy(bf16[32,256,256]{2,1,0:T(8,128)(2,1)} %bitcast.108) | data formatting | bytes 8388608 | tf_op jit(solution)/shard_map/squeeze | solution.py:112
  20.8 0.0 copy-start.5
  20.8 0.0 copy-start.4
  20.8 87.6 %all-to-all-done = bf16[32,256,256]{1,0,2:T(8,128)(2,1)} async-done(((bf16[32,256,256]{1,0,2:T(8,128)(2,1)}), bf16[32,256,256]{1,0,2:T(8,128)(2,1)}, u32[]{:S(2)}, u32[]{:S(2)}) %all-to-all-start) | async-done | bytes 4194336 | tf_op jit(solution)/shard_map/all_to_all | solution.py:119
  108.4 4.8 %all-to-all-start.2 = ((bf16[32,256,256]{2,0,1:T(8,128)(2,1)}), bf16[32,256,256]{2,0,1:T(8,128)(2,1)}, u32[]{:S(2)}, u32[]{:S(2)}) async-start(bf16[32,256,256]{2,0,1:T(8,128)(2,1)} %copy.98), calls=%async_computation.2 | async-start | bytes 8388608 | tf_op jit(solution)/shard_map/all_to_all | solution.py:120
  113.1 0.0 copy-done.5
  113.2 0.0 copy-done
  113.2 0.6 gather_fusion
  113.8 0.6 gather_fusion.1
  114.3 0.0 copy-done.4
  114.4 0.6 fusion.41
  115.0 6.8 %copy.81 = bf16[8,32,256,32]{2,3,1,0:T(8,128)(2,1)} copy(bf16[8,32,256,32]{2,1,3,0:T(8,128)(2,1)} %bitcast.11) | data formatting | bytes 8388608 | tf_op jit(solution)/shard_map/all_to_all | solution.py:119
  121.7 9.7 %fusion.6 = f32[256,256,32]{1,0,2:T(8,128)} fusion(bf16[256,256,32]{1,2,0:T(8,128)(2,1)} %bitcast.100, bf16[4,256,256]{2,1,0:T(8,128)(2,1)S(1)} %gather_fusion.1, bf16[4,256,256]{2,1,0:T(8,128)(2,1)S(1)} %gather_fusion), kind=kOutput, calls=%fused_computation.10 | convolution fusion | flops 2149580800 | bytes 12845056 | tf_op jit(solution)/shard_map/lk,lsu->ksu/dot_general | solution.py:126
  131.4 9.7 %fusion.8 = f32[256,256,32]{1,0,2:T(8,128)} fusion(bf16[256,256,32]{1,2,0:T(8,128)(2,1)} %bitcast.101, bf16[4,256,256]{2,1,0:T(8,128)(2,1)S(1)} %gather_fusion.1, bf16[4,256,256]{2,1,0:T(8,128)(2,1)S(1)} %gather_fusion), kind=kOutput, calls=%fused_computation.12 | convolution fusion | flops 2149580800 | bytes 12845056 | tf_op jit(solution)/shard_map/lk,lsu->ksu/dot_general | solution.py:126
  141.1 9.9 %fusion.4 = f32[256,256,32]{1,0,2:T(8,128)} fusion(bf16[256,256,32]{1,2,0:T(8,128)(2,1)} %bitcast.102, bf16[4,256,256]{2,1,0:T(8,128)(2,1)S(1)} %gather_fusion.1, bf16[4,256,256]{2,1,0:T(8,128)(2,1)S(1)} %gather_fusion), kind=kOutput, calls=%fused_computation.8 | convolution fusion | flops 2149580800 | bytes 12845056 | tf_op jit(solution)/shard_map/lk,lsu->ksu/dot_general | solution.py:126
  151.0 16.7 %add_convert_fusion = bf16[256,256,32]{1,0,2:T(8,128)(2,1)} fusion(f32[256,256,32]{1,0,2:T(8,128)} %fusion.4, f32[256,256,32]{1,0,2:T(8,128)} %fusion.6, f32[256,256,32]{1,0,2:T(8,128)} %fusion.8, f32[]{:T(128)} %bitcast.26, f32[]{:T(128)} %bitcast.20, f32[]{:T(128)} %bitcast.14, f32[]{:T(128)} %bitcast, bf16[256,256,32]{1,2,0:T(8,128)(2,1)} %bitcast.103, ...), kind=kOutput, calls=%fused_computation.4 | convolution fusion | flops 2166358016 | bytes 33816592 | tf_op jit(solution)/shard_map/lk,lsu->ksu/dot_general | solution.py:126
  167.7 7.8 %copy.96 = bf16[256,256,32]{0,2,1:T(8,128)(2,1)} copy(bf16[256,256,32]{1,0,2:T(8,128)(2,1)} %add_convert_fusion) | data formatting | bytes 8388608 | tf_op jit(solution)/shard_map/convert_element_type | solution.py:130
  175.5 31.4 %all-to-all-done.2 = bf16[32,256,256]{2,0,1:T(8,128)(2,1)} async-done(((bf16[32,256,256]{2,0,1:T(8,128)(2,1)}), bf16[32,256,256]{2,0,1:T(8,128)(2,1)}, u32[]{:S(2)}, u32[]{:S(2)}) %all-to-all-start.2) | async-done | bytes 4194336 | tf_op jit(solution)/shard_map/all_to_all | solution.py:120
  206.9 4.6 %all-to-all-start.1 = ((bf16[256,256,32]{0,2,1:T(8,128)(2,1)}), bf16[256,256,32]{0,2,1:T(8,128)(2,1)}, u32[]{:S(2)}, u32[]{:S(2)}) async-start(bf16[256,256,32]{0,2,1:T(8,128)(2,1)} %copy.96), calls=%async_computation.1 | async-start | bytes 8388608 | tf_op jit(solution)/shard_map/all_to_all | solution.py:129
  211.5 6.7 %copy.100 = bf16[8,32,32,256]{3,2,1,0:T(8,128)(2,1)} copy(bf16[8,32,32,256]{3,1,2,0:T(8,128)(2,1)} %bitcast.38) | data formatting | bytes 8388608 | tf_op jit(solution)/shard_map/all_to_all | solution.py:120
  218.2 87.3 %all-to-all-done.1 = bf16[256,256,32]{0,2,1:T(8,128)(2,1)} async-done(((bf16[256,256,32]{0,2,1:T(8,128)(2,1)}), bf16[256,256,32]{0,2,1:T(8,128)(2,1)}, u32[]{:S(2)}, u32[]{:S(2)}) %all-to-all-start.1) | async-done | bytes 4194336 | tf_op jit(solution)/shard_map/all_to_all | solution.py:129
  305.5 0.0 copy-start.2
  305.5 2.8 copy.97
  308.3 0.0 copy-start.3
  308.3 0.6 copy-done.2
  308.9 6.3 %fusion.14 = f32[256,256,1]{0,1,2:T(8,128)} fusion(bf16[256,32,256]{0,2,1:T(8,128)(2,1)S(1)} %bitcast.106, bf16[256,32,256]{2,1,0:T(8,128)(2,1)S(1)} %bitcast.105), kind=kOutput, calls=%fused_computation.18 | convolution fusion | flops 1073741824 | bytes 8650752 | tf_op jit(solution)/shard_map/lsu,lsv->uv/dot_general | solution.py:132
  315.2 0.0 copy-done.3
  315.2 31.1 %shard_map.64 = bf16[256,256]{1,0:T(8,128)(2,1)} custom-call(f32[8,32,256]{2,1,0:T(8,128)} %bitcast.111, bf16[32,256]{1,0:T(8,128)(2,1)} %bitcast.112, f32[8,32,256]{2,1,0:T(8,128)} %bitcast.110), custom_call_target="tpu_custom_call" | custom-call | tf_op jit(solution)/shard_map/pallas_call | solution.py:92
  346.3 0.0 copy-start.1
  346.3 8.8 %fusion.1 = bf16[1,256,32,256]{1,3,2,0:T(8,128)(2,1)} fusion(bf16[256,32,256]{0,2,1:T(8,128)(2,1)} %bitcast.107, bf16[256,32,256]{2,1,0:T(8,128)(2,1)} %bitcast.104, bf16[256,256]{1,0:T(8,128)(2,1)} %shard_map.64), kind=kOutput, calls=%fused_computation.5 | convolution fusion | flops 1080033280 | bytes 12713984 | tf_op jit(solution)/shard_map/lsu,uv->lsv/dot_general | solution.py:134
  355.1 7.8 %copy.105 = bf16[1,256,32,256]{3,2,1,0:T(8,128)(2,1)} copy(bf16[1,256,32,256]{1,3,2,0:T(8,128)(2,1)} %fusion.1) | data formatting | bytes 8388608 | tf_op jit(solution)/shard_map/broadcast_in_dim | solution.py:137
  362.9 0.0 copy-done.1
  (2 shorter events, 0.0 us)
Async XLA Ops:
  0.0 113.2 %copy-start = (bf16[8,256,256]{2,1,0:T(8,128)(2,1)S(1)}, bf16[8,256,256]{2,1,0:T(8,128)(2,1)}, u32[]{:S(2)}) copy-start(bf16[8,256,256]{2,1,0:T(8,128)(2,1)} %param.7) | copy-start | bytes 3145732
  7.9 100.4 %all-to-all-start = ((bf16[32,256,256]{1,0,2:T(8,128)(2,1)}), bf16[32,256,256]{1,0,2:T(8,128)(2,1)}, u32[]{:S(2)}, u32[]{:S(2)}) async-start(bf16[32,256,256]{1,0,2:T(8,128)(2,1)} %bitcast.109), calls=%async_computation | async-start | bytes 8388608 | tf_op jit(solution)/shard_map/all_to_all | solution.py:119
  20.8 92.4 %copy-start.5 = (s32[1,4,2]{1,2,0:T(2,128)S(1)}, s32[1,4,2]{1,2,0:T(2,128)}, u32[]{:S(2)}) copy-start(s32[1,4,2]{1,2,0:T(2,128)} %param.8) | copy-start | bytes 100
  20.8 93.6 %copy-start.4 = (f32[1,4]{1,0:T(1,128)S(1)}, f32[1,4]{1,0:T(1,128)}, u32[]{:S(2)}) copy-start(f32[1,4]{1,0:T(1,128)} %param.9) | copy-start | bytes 52
  108.4 98.6 %all-to-all-start.2 = ((bf16[32,256,256]{2,0,1:T(8,128)(2,1)}), bf16[32,256,256]{2,0,1:T(8,128)(2,1)}, u32[]{:S(2)}, u32[]{:S(2)}) async-start(bf16[32,256,256]{2,0,1:T(8,128)(2,1)} %copy.98), calls=%async_computation.2 | async-start | bytes 8388608 | tf_op jit(solution)/shard_map/all_to_all | solution.py:120
  206.9 98.5 %all-to-all-start.1 = ((bf16[256,256,32]{0,2,1:T(8,128)(2,1)}), bf16[256,256,32]{0,2,1:T(8,128)(2,1)}, u32[]{:S(2)}, u32[]{:S(2)}) async-start(bf16[256,256,32]{0,2,1:T(8,128)(2,1)} %copy.96), calls=%async_computation.1 | async-start | bytes 8388608 | tf_op jit(solution)/shard_map/all_to_all | solution.py:129
  305.5 3.4 copy-start.2
  308.3 6.9 %copy-start.3 = (bf16[256,32,8,32]{0,3,2,1:T(8,128)(2,1)}, bf16[256,32,8,32]{0,3,2,1:T(8,128)(2,1)S(1)}, u32[]{:S(2)}) copy-start(bf16[256,32,8,32]{0,3,2,1:T(8,128)(2,1)S(1)} %copy.97) | copy-start | bytes 12582916
  346.3 16.7 %copy-start.1 = (bf16[8,256,256]{2,1,0:T(8,128)(2,1)S(1)}, bf16[8,256,256]{2,1,0:T(8,128)(2,1)}, u32[]{:S(2)}) copy-start(bf16[8,256,256]{2,1,0:T(8,128)(2,1)} %param.7) | copy-start | bytes 3145732

commit v2 on v1

--- a/solution.py
+++ b/solution.py
@@ -108,18 +108,167 @@
     )(env_part.reshape(n, rows, bond), parent_block, top_env.reshape(n, rows, width))
 
 
-def shards(child_tensors, leg_ops, term_ops, term_coef, parent, top_env):
-    tensor = child_tensors[0]
+CHUNK = 32
+GROUP = 8
+
+
+def core_kernel(
+    n, number, tens_ref, rc_ref, coef_ref, left_ref, tsel_ref, loc_ref,
+    full, image, stage_t, stage_l, own_sem, ssem, fsem, esem, rsem, xsem,
+):
+    me = lax.axis_index("shard")
+    cores = 2
+    chips = n // cores
+    chip, core = me // cores, lax.rem(me, cores)
+    rows = tens_ref.shape[1]
+    half = full.shape[0]
+    steps = half // CHUNK
+    side = lax.rem(chip, 2)
+    twin = chip * cores + 1 - core
+    mate = (chip + 1 - 2 * side) * cores + core
+    others = [lax.rem(chip + k, chips) for k in range(1, chips)]
+
+    barrier = pltpu.get_barrier_semaphore()
+    for k in range(1, n):
+        pl.semaphore_signal(
+            barrier, inc=1, device_id={"shard": lax.rem(me + k, n)}, device_id_type=MESH
+        )
+    pl.semaphore_wait(barrier, n - 1)
+
+    def place(q, j):
+        return full.at[pl.ds(q * CHUNK, CHUNK), pl.ds(pl.multiple_of(j * rows, rows), rows), :]
+
+    def source(q, which):
+        return tens_ref.at[pl.ds(which * half + q * CHUNK, CHUNK)]
+
+    def remote(src, dst, send, recv, j):
+        return pltpu.make_async_remote_copy(
+            src_ref=src, dst_ref=dst, send_sem=send, recv_sem=recv,
+            device_id={"shard": j}, device_id_type=MESH,
+        )
+
+    sent = []
+    local_copies = []
+    for q in range(steps):
+        for z in others:
+            copy = remote(
+                source(q, lax.rem(z, 2)), place(q, me), ssem.at[q, z], rsem.at[q, me],
+                z * cores + core,
+            )
+            copy.start()
+            sent.append(copy)
+        copy = remote(source(q, side), place(q, me), fsem.at[q, chip], rsem.at[q, me], twin)
+        copy.start()
+        sent.append(copy)
+        copy = pltpu.make_async_copy(source(q, side), place(q, me), own_sem.at[q])
+        copy.start()
+        local_copies.append(copy)
+
+    for q in range(steps):
+        for z in others:
+            j = z * cores + core
+            remote(place(q, j), place(q, j), ssem.at[q, z], rsem.at[q, j], twin).wait_recv()
+            copy = remote(place(q, j), place(q, j), fsem.at[q, z], rsem.at[q, j], twin)
+            copy.start()
+            sent.append(copy)
+        local_copies[q].wait()
+        for z in [chip] + others:
+            j = z * cores + 1 - core
+            remote(place(q, j), place(q, j), fsem.at[q, z], rsem.at[q, j], twin).wait_recv()
+
+        def block(g, _):
+            first = q * CHUNK + g * GROUP
+            goal = side * half + first
+            for i in range(GROUP):
+                made = lax.dot_general(
+                    rc_ref[...], full[first + i], (((1,), (1,)), ((), ())),
+                    preferred_element_type=jnp.float32,
+                )
+                made = (made * coef_ref[...]).astype(jnp.bfloat16)
+                for t in range(number):
+                    image[t, pl.ds(i * 2 * rows, 2 * rows), :] = made[
+                        t * 2 * rows : (t + 1) * 2 * rows
+                    ]
+                base = number * 2 * rows
+                tsel_ref[goal + i] = made[base : base + rows]
+                stage_t[first + i] = made[base + rows : base + 2 * rows]
+            total = jnp.dot(image[0], left_ref[0], preferred_element_type=jnp.float32)
+            for t in range(1, number):
+                total += jnp.dot(image[t], left_ref[t], preferred_element_type=jnp.float32)
+            total = total.astype(jnp.bfloat16).reshape(GROUP, 2 * rows, total.shape[-1])
+            loc_ref[pl.ds(goal, GROUP)] = total[:, :rows]
+            stage_l[pl.ds(first, GROUP)] = total[:, rows:]
+            return 0
+
+        lax.fori_loop(0, CHUNK // GROUP, block, 0)
+        here = pl.ds(q * CHUNK, CHUNK)
+        there = pl.ds(side * half + q * CHUNK, CHUNK)
+        for which, (stage, goal_ref) in enumerate(((stage_t, tsel_ref), (stage_l, loc_ref))):
+            copy = remote(
+                stage.at[here], goal_ref.at[there], esem.at[which, q], xsem.at[which, q], mate
+            )
+            copy.start()
+            sent.append(copy)
+    for q in range(steps):
+        far = pl.ds((1 - side) * half + q * CHUNK, CHUNK)
+        for which, goal_ref in enumerate((tsel_ref, loc_ref)):
+            remote(
+                goal_ref.at[far], goal_ref.at[far], esem.at[which, q], xsem.at[which, q], mate
+            ).wait_recv()
+    for copy in sent:
+        copy.wait_send()
+
+
+def local_of(tensor, left_ops, right_ops, weights):
+    n = lax.axis_size("shard")
+    me = lax.axis_index("shard")
+    rows, bond = tensor.shape[0], tensor.shape[1]
+    number = weights.shape[0]
+    half = bond // 2
+    steps = half // CHUNK
+    chip = me // 2
+    mate = (chip + 1 - 2 * (chip % 2)) * 2 + me % 2
+    pair = jnp.stack([me, mate])
+    slabs = jnp.swapaxes(right_ops, 1, 2).reshape(number, n, rows, bond)
+    chosen = slabs[:, pair]
+    wanted = pair[:, None] * rows + jnp.arange(rows)[None, :]
+    onehot = (wanted[:, :, None] == jnp.arange(bond)).astype(jnp.bfloat16)
+    rc = jnp.concatenate([chosen, onehot[None]], axis=0).reshape((number + 1) * 2 * rows, bond)
+    coef = jnp.repeat(jnp.concatenate([weights, jnp.ones((1,), jnp.float32)]), 2 * rows)[:, None]
+    upward = jnp.transpose(tensor, (2, 0, 1))
+    vmem = pl.BlockSpec(memory_space=pltpu.VMEM)
+    hbm = pl.BlockSpec(memory_space=pl.ANY)
+    slab = jax.ShapeDtypeStruct((bond, rows, bond), jnp.bfloat16)
+    dma = pltpu.SemaphoreType.DMA
+    return pl.pallas_call(
+        functools.partial(core_kernel, n, number),
+        out_shape=(slab, slab),
+        in_specs=[hbm, vmem, vmem, vmem],
+        out_specs=(vmem, vmem),
+        scratch_shapes=[
+            pltpu.VMEM((half, bond, bond), jnp.bfloat16),
+            pltpu.VMEM((number, GROUP * 2 * rows, bond), jnp.bfloat16),
+            pltpu.VMEM((half, rows, bond), jnp.bfloat16),
+            pltpu.VMEM((half, rows, bond), jnp.bfloat16),
+            dma((steps,)),
+            dma((steps, n // 2)),
+            dma((steps, n // 2)),
+            dma((2, steps)),
+            dma((steps, n)),
+            dma((2, steps)),
+        ],
+        compiler_params=pltpu.CompilerParams(
+            collective_id=1, has_side_effects=True, vmem_limit_bytes=56 * 1024 * 1024
+        ),
+    )(upward, rc, coef, left_ops)
+
+
+def by_exchange(tensor, left_ops, right_ops, weights):
     bond = tensor.shape[1]
-    picks = term_ops[0]
-    weights = term_coef[0]
-    number = weights.shape[0]
-    left_ops = leg_ops[picks[:, 0]]
-    right_ops = leg_ops[picks[:, 1]]
     upward = lax.all_to_all(tensor, "shard", split_axis=2, concat_axis=0, tiled=True)
     regrouped = lax.all_to_all(tensor, "shard", split_axis=1, concat_axis=0, tiled=True)
     summed = jnp.zeros((bond, bond, upward.shape[2]), jnp.float32)
-    for term in range(number):
+    for term in range(weights.shape[0]):
         image = jnp.einsum(
             "lru,rs->lsu", upward, right_ops[term], preferred_element_type=jnp.float32
         ).astype(jnp.bfloat16)
@@ -129,10 +278,21 @@
     local = lax.all_to_all(
         summed.astype(jnp.bfloat16), "shard", split_axis=1, concat_axis=2, tiled=True
     )
-    env_part = jnp.einsum("lsu,lsv->uv", regrouped, local, preferred_element_type=jnp.float32)
+    return jnp.transpose(regrouped, (2, 1, 0)), jnp.transpose(local, (2, 1, 0))
+
+
+def shards(child_tensors, leg_ops, term_ops, term_coef, parent, top_env):
+    tensor = child_tensors[0]
+    picks = term_ops[0]
+    weights = term_coef[0]
+    left_ops = leg_ops[picks[:, 0]]
+    right_ops = leg_ops[picks[:, 1]]
+    form = local_of if tensor.shape[0] % 16 == 0 else by_exchange
+    slab, local = form(tensor, left_ops, right_ops, weights)
+    env_part = jnp.einsum("usl,vsl->uv", slab, local, preferred_element_type=jnp.float32)
     hole = hole_of(env_part, parent[0], top_env)
-    result = local.astype(jnp.float32) + jnp.einsum(
-        "lsu,uv->lsv", regrouped, hole, preferred_element_type=jnp.float32
+    result = jnp.transpose(local, (2, 1, 0)).astype(jnp.float32) + jnp.einsum(
+        "usl,uv->lsv", slab, hole, preferred_element_type=jnp.float32
     )
     return result.astype(jnp.bfloat16)[None]
 

time: 364 us -> 317 us (0.87)
  Pallas kernels: 31.1 us -> 268 us
  waiting for transfers between devices: 206 us -> 0 us
  matrix products: 61 us -> 18.6 us
  local copies, waits for them, and re-layouts: 48.7 us -> 20.7 us
  starting transfers between devices: 15.7 us -> 0 us
  other arithmetic: 0.01 us -> 8.73 us
    pallas_call x0 -> x1, Pallas kernels: none -> 237 us  [local_of(): pl.pallas_call(functools.partial(core_kernel, n, number), out_shape=(slab...]
    all_to_all x3 -> x0, waiting for transfers between devices: 206 us -> none  [the longest x1 87.6 us: shards(): lax.all_to_all(tensor, 'shard', split_axis=2, concat_axis=0, tiled=True)]
    dot_general x6 -> x2, matrix products: 61 us -> 18.6 us  [the longest x1 12.9 us: shards(): jnp.einsum('usl,vsl->uv', slab, local, preferred_element_type=jnp.float32)]
    all_to_all x3 -> x0, local copies, waits for them, and re-layouts: 16.3 us -> none  [the longest x1 6.76 us: shards(): lax.all_to_all(tensor, 'shard', split_axis=2, concat_axis=0, tiled=True)]
    all_to_all x3 -> x0, starting transfers between devices: 15.7 us -> none  [the longest x1 6.35 us: shards(): lax.all_to_all(tensor, 'shard', split_axis=2, concat_axis=0, tiled=True)]
    convert_element_type x1 -> x0, local copies, waits for them, and re-layouts: 7.83 us -> none  [shards(): summed.astype(jnp.bfloat16)]
    broadcast_in_dim x0 -> x1, other arithmetic: none -> 6.83 us  [shards(): return result.astype(jnp.bfloat16)[None]]
    squeeze x1 -> x0, local copies, waits for them, and re-layouts: 6.48 us -> none  [shards(): tensor = child_tensors[0]]
  transfers between devices with their start and end apart: 3 -> 0, of which waited for: 3 -> 0; matrix products, arithmetic and copies ran while one was open for 21% -> 0% of each run, Pallas kernels for 0% -> 0%
where the time goes in v2:
time: 317 us; the launch traced here: 316 us
  Pallas kernels  268 us (85%)
  local copies, waits for them, and re-layouts  20.7 us (7%)
  matrix products  18.6 us (6%)
  other arithmetic  8.73 us (3%)
    pallas_call x1, Pallas kernels, local_of(): pl.pallas_call(functools.partial(core_kernel, n, number), out_shape=(slab...  237 us
    pallas_call x1, Pallas kernels, hole_of(): pl.pallas_call(functools.partial(tail_kernel, n, nc, bond, factor), out_s...  31.4 us
    dot_general x1, matrix products, shards(): jnp.einsum('usl,vsl->uv', slab, local, preferred_element_type=jnp.float32)  12.9 us
    broadcast_in_dim x1, local copies, waits for them, and re-layouts, shards(): return result.astype(jnp.bfloat16)[None]  8.49 us
    unnamed x5, local copies, waits for them, and re-layouts  7.84 us
    broadcast_in_dim x1, other arithmetic, shards(): return result.astype(jnp.bfloat16)[None]  6.83 us

profile of v2, /device:TPU:0, one launch (start us, length us, event | category | flops | bytes accessed | tf_op | source)
XLA Modules:
  0.0 316.2 jit_solution(3207668112130565060)
XLA Ops:
  0.0 0.0 copy-start
  0.0 0.8 pad_maximum_fusion.1
  0.8 0.1 fusion.10
  0.9 0.1 add_multiply_fusion
  1.0 0.1 iota_add_fusion
  1.0 0.8 fusion.11
  1.8 0.1 broadcast_in_dim.4
  1.9 0.1 fusion.8
  2.0 0.8 broadcast_in_dim_reshape.4.coef_ref
  2.8 0.0 copy-done
  2.8 1.4 gather_fusion.2
  4.2 0.6 gather_fusion
  4.8 0.2 copy.24
  5.0 0.6 gather_fusion.1
  5.6 0.7 copy.25
  6.3 7.8 %copy.23 = bf16[1,32,256,256]{2,1,3,0:T(8,128)(2,1)} copy(bf16[1,32,256,256]{3,2,1,0:T(8,128)(2,1)} %param.6) | data formatting | bytes 8388608 | tf_op args[0]
  14.1 236.7 %shard_map.64 = (bf16[256,32,256]{2,1,0:T(8,128)(2,1)}, bf16[256,32,256]{2,1,0:T(8,128)(2,1)}) custom-call(bf16[256,32,256]{2,1,0:T(8,128)(2,1)} %bitcast.31, bf16[320,256]{1,0:T(8,128)(2,1)} %bitcast.34, f32[320,1]{1,0:T(8,128)} %broadcast_in_dim_reshape.4.coef_ref, bf16[4,256,256]{2,1,0:T(8,128)(2,1)} %gather_fusion.2), custom_call_target="tpu_custom_call" | custom-call | tf_op jit(solution)/shard_map/pallas_call | solution.py:243
  250.9 12.9 %fusion.2 = f32[256,256,1]{1,0,2:T(8,128)} fusion(bf16[256,32,256]{2,1,0:T(8,128)(2,1)} %get-tuple-element.7, bf16[256,32,256]{2,1,0:T(8,128)(2,1)} %get-tuple-element.8), kind=kOutput, calls=%fused_computation.6 | convolution fusion | flops 1073741824 | bytes 8650752 | tf_op jit(solution)/shard_map/usl,vsl->uv/dot_general | solution.py:292
  263.8 31.4 %shard_map.65 = bf16[256,256]{1,0:T(8,128)(2,1)} custom-call(f32[8,32,256]{2,1,0:T(8,128)} %bitcast.37, bf16[32,256]{1,0:T(8,128)(2,1)} %bitcast.38, f32[8,32,256]{2,1,0:T(8,128)} %bitcast.36), custom_call_target="tpu_custom_call" | custom-call | tf_op jit(solution)/shard_map/pallas_call | solution.py:92
  295.2 0.0 copy-start.1
  295.2 5.7 %fusion.4 = f32[256,32,256]{2,0,1:T(8,128)S(1)} fusion(bf16[256,32,256]{2,1,0:T(8,128)(2,1)} %get-tuple-element.8, bf16[256,256]{1,0:T(8,128)(2,1)} %shard_map.65), kind=kOutput, calls=%fused_computation.8 | convolution fusion | flops 1073741824 | bytes 12713984 | tf_op jit(solution)/shard_map/usl,uv->lsv/dot_general | solution.py:294
  300.9 0.0 copy-done.1
  300.9 6.8 %fusion.1 = bf16[1,256,32,256]{1,2,3,0:T(8,128)(2,1)} fusion(f32[256,32,256]{2,0,1:T(8,128)S(1)} %fusion.4, bf16[256,32,256]{2,1,0:T(8,128)(2,1)S(1)} %copy-done.1), kind=kLoop, calls=%fused_computation.5 | loop fusion | flops 6291456 | bytes 16777216 | tf_op jit(solution)/shard_map/broadcast_in_dim | solution.py:297
  307.7 8.5 %copy.32 = bf16[1,256,32,256]{3,2,1,0:T(8,128)(2,1)} copy(bf16[1,256,32,256]{1,2,3,0:T(8,128)(2,1)} %fusion.1) | data formatting | bytes 8388608 | tf_op jit(solution)/shard_map/broadcast_in_dim | solution.py:297
  (3 shorter events, 0.0 us)
Async XLA Ops:
  0.0 2.8 copy-start
  295.2 5.7 %copy-start.1 = (bf16[256,32,256]{2,1,0:T(8,128)(2,1)S(1)}, bf16[256,32,256]{2,1,0:T(8,128)(2,1)}, u32[]{:S(2)}) copy-start(bf16[256,32,256]{2,1,0:T(8,128)(2,1)} %get-tuple-element.7) | copy-start | bytes 12582916

commit v3 on v1

--- a/solution.py
+++ b/solution.py
@@ -45,18 +45,18 @@
     sent = [send(0, env_ref.at[j], envv.at[me], "shard", j, me) for j in peers]
     sent += [send(1, par_ref, parv.at[me], "shard", j, me) for j in peers]
     parv[me] = par_ref[...]
-    total = env_ref[me]
+    total = env_ref[me].astype(jnp.float32)
     for j in peers:
         arrive(0, envv.at[j], "shard", j)
-        total = total + envv[j]
-    envf[me] = total
+        total = total + envv[j].astype(jnp.float32)
+    envf[me] = total.astype(jnp.bfloat16)
     sent += [send(2, envf.at[me], envf.at[me], "shard", j, me) for j in peers]
     for j in peers:
         arrive(1, parv.at[j], "shard", j)
     lift = parv[...].astype(jnp.float32).reshape(n * rows, width)
     for j in peers:
         arrive(2, envf.at[j], "shard", j)
-    env = envf[...].reshape(n * rows, width) * (1.0 / bond)
+    env = envf[...].astype(jnp.float32).reshape(n * rows, width) * (1.0 / bond)
     half = jnp.dot(env, lift, precision=HIGH, preferred_element_type=jnp.float32)
     lifted = lax.dot_general(
         lift, half, (((0,), (0,)), ((), ())), precision=HIGH, preferred_element_type=jnp.float32
@@ -67,11 +67,11 @@
     for j in kids:
         arrive(3, chv.at[j], "child", j)
         slab = slab + chv[j]
-    cpf[me] = slab
+    cpf[me] = slab.astype(jnp.bfloat16)
     sent += [send(4, cpf.at[me], cpf.at[me], "shard", j, me) for j in peers]
     for j in peers:
         arrive(4, cpf.at[j], "shard", j)
-    coupling = cpf[...].reshape(n * rows, width)
+    coupling = cpf[...].astype(jnp.float32).reshape(n * rows, width)
     half = jnp.dot(lift, coupling, precision=HIGH, preferred_element_type=jnp.float32)
     hole = lax.dot_general(
         half, lift, (((1,), (1,)), ((), ())), precision=HIGH, preferred_element_type=jnp.float32
@@ -96,30 +96,213 @@
         out_specs=vmem,
         scratch_shapes=[
             block(n, jnp.bfloat16),
-            block(n, jnp.float32),
-            block(n, jnp.float32),
+            block(n, jnp.bfloat16),
+            block(n, jnp.bfloat16),
             block(n, jnp.float32),
             block(nc, jnp.float32),
-            block(n, jnp.float32),
+            block(n, jnp.bfloat16),
             pltpu.SemaphoreType.DMA((5, most)),
             pltpu.SemaphoreType.DMA((5, most)),
         ],
         compiler_params=pltpu.CompilerParams(collective_id=0, has_side_effects=True),
-    )(env_part.reshape(n, rows, bond), parent_block, top_env.reshape(n, rows, width))
-
-
-def shards(child_tensors, leg_ops, term_ops, term_coef, parent, top_env):
-    tensor = child_tensors[0]
+    )(env_part.astype(jnp.bfloat16).reshape(n, rows, bond), parent_block, top_env.reshape(n, rows, width))
+
+
+CHUNK = 16
+GROUP = 8
+LINE = 4
+
+
+def core_kernel(
+    n, number, tens_ref, rc_ref, coef_ref, left_ref, tsel_ref, loc_ref,
+    full, image, stage_t, stage_l, own_sem, csem, fsem, esem, rsem, xsem,
+):
+    me = lax.axis_index("shard")
+    cores = n // LINE
+    chip, core = me // cores, lax.rem(me, cores)
+    rows = tens_ref.shape[1]
+    steps = tens_ref.shape[0] // CHUNK
+    other = 1 - core
+    mate_chip = chip + 1 - 2 * lax.rem(chip, 2)
+    twin = chip * cores + other
+    mate = mate_chip * cores + core
+    across = (LINE - 1 - chip) * cores + core
+    far = (LINE - 1 - mate_chip) * cores + core
+    middle = jnp.logical_or(chip == 1, chip == 2)
+    edge = jnp.logical_or(chip == 0, chip == 3)
+
+    barrier = pltpu.get_barrier_semaphore()
+    for k in range(1, n):
+        pl.semaphore_signal(
+            barrier, inc=1, device_id={"shard": lax.rem(me + k, n)}, device_id_type=MESH
+        )
+    pl.semaphore_wait(barrier, n - 1)
+
+    def span(q):
+        return pl.ds(pl.multiple_of(q * CHUNK, CHUNK), CHUNK)
+
+    def place(q, j):
+        return full.at[span(q), pl.ds(pl.multiple_of(j * rows, rows), rows), :]
+
+    def remote(src, dst, send, recv, j):
+        return pltpu.make_async_remote_copy(
+            src_ref=src, dst_ref=dst, send_sem=send, recv_sem=recv,
+            device_id={"shard": j}, device_id_type=MESH,
+        )
+
+    def own_to(q, send, j):
+        return remote(tens_ref.at[span(q)], place(q, me), send, rsem.at[q, me], j)
+
+    def pass_on(q, j, send, goal):
+        return remote(place(q, j), place(q, j), send, rsem.at[q, j], goal)
+
+    def finished(which, q):
+        stage, goal_ref = ((stage_t, tsel_ref), (stage_l, loc_ref))[which]
+        return remote(
+            stage.at[span(q)], goal_ref.at[span(q)], esem.at[which, q], xsem.at[which, q], mate
+        )
+
+    def kept(q):
+        return pltpu.make_async_copy(tens_ref.at[span(q)], place(q, me), own_sem.at[q])
+
+    def loop(count, body):
+        def step(q, _):
+            body(q)
+            return 0
+
+        lax.fori_loop(0, count, step, 0)
+
+    @pl.when(edge)
+    def _():
+        loop(steps, lambda q: own_to(q, csem.at[0, q], mate).start())
+
+        def take(q):
+            own_to(q, csem.at[0, q], mate).wait_send()
+            for which in range(2):
+                finished(which, q).wait_recv()
+
+        loop(steps, take)
+
+    @pl.when(middle)
+    def _():
+        def begin(q):
+            own_to(q, fsem.at[0, q], twin).start()
+            kept(q).start()
+
+        loop(steps, begin)
+
+        def relay(q):
+            own_to(q, csem.at[0, q], across).start()
+            pass_on(q, mate, csem.at[1, q], twin).wait_recv()
+            pass_on(q, mate, csem.at[1, q], across).start()
+            pass_on(q, mate, fsem.at[1, q], twin).start()
+
+        relay(0)
+        relay(1)
+
+        def chunk(q):
+            @pl.when(q + 2 < steps)
+            def _():
+                relay(q + 2)
+
+            for slot, j in ((2, across), (3, far)):
+                pass_on(q, j, fsem.at[slot, q], twin).wait_recv()
+                pass_on(q, j, fsem.at[slot, q], twin).start()
+            kept(q).wait()
+            for slot, j in enumerate((me, mate, across, far)):
+                pass_on(q, j + other - core, fsem.at[slot, q], twin).wait_recv()
+
+            def block(g, _):
+                first = q * CHUNK + g * GROUP
+                for i in range(GROUP):
+                    made = lax.dot_general(
+                        rc_ref[...], full[first + i], (((1,), (1,)), ((), ())),
+                        preferred_element_type=jnp.float32,
+                    )
+                    made = (made * coef_ref[...]).astype(jnp.bfloat16)
+                    for t in range(number):
+                        image[t, pl.ds(i * 2 * rows, 2 * rows), :] = made[
+                            t * 2 * rows : (t + 1) * 2 * rows
+                        ]
+                    base = number * 2 * rows
+                    tsel_ref[first + i] = made[base : base + rows]
+                    stage_t[first + i] = made[base + rows : base + 2 * rows]
+                total = jnp.dot(image[0], left_ref[0], preferred_element_type=jnp.float32)
+                for t in range(1, number):
+                    total += jnp.dot(image[t], left_ref[t], preferred_element_type=jnp.float32)
+                total = total.astype(jnp.bfloat16).reshape(GROUP, 2 * rows, total.shape[-1])
+                loc_ref[pl.ds(first, GROUP)] = total[:, :rows]
+                stage_l[pl.ds(first, GROUP)] = total[:, rows:]
+                return 0
+
+            lax.fori_loop(0, CHUNK // GROUP, block, 0)
+            for which in range(2):
+                finished(which, q).start()
+
+        loop(steps, chunk)
+
+        def drain(q):
+            own_to(q, fsem.at[0, q], twin).wait_send()
+            own_to(q, csem.at[0, q], across).wait_send()
+            pass_on(q, mate, csem.at[1, q], across).wait_send()
+            for slot, j in ((1, mate), (2, across), (3, far)):
+                pass_on(q, j, fsem.at[slot, q], twin).wait_send()
+            for which in range(2):
+                finished(which, q).wait_send()
+
+        loop(steps, drain)
+
+
+def local_of(tensor, left_ops, right_ops, weights):
+    n = lax.axis_size("shard")
+    me = lax.axis_index("shard")
+    rows, bond = tensor.shape[0], tensor.shape[1]
+    number = weights.shape[0]
+    steps = bond // CHUNK
+    cores = n // LINE
+    chip = me // cores
+    mate = (chip + 1 - 2 * (chip % 2)) * cores + me % cores
+    pair = jnp.stack([me, mate])
+    slabs = jnp.swapaxes(right_ops, 1, 2).reshape(number, n, rows, bond)
+    chosen = slabs[:, pair]
+    wanted = pair[:, None] * rows + jnp.arange(rows)[None, :]
+    onehot = (wanted[:, :, None] == jnp.arange(bond)).astype(jnp.bfloat16)
+    rc = jnp.concatenate([chosen, onehot[None]], axis=0).reshape((number + 1) * 2 * rows, bond)
+    coef = jnp.repeat(jnp.concatenate([weights, jnp.ones((1,), jnp.float32)]), 2 * rows)[:, None]
+    upward = jnp.transpose(tensor, (2, 0, 1))
+    vmem = pl.BlockSpec(memory_space=pltpu.VMEM)
+    hbm = pl.BlockSpec(memory_space=pl.ANY)
+    slab = jax.ShapeDtypeStruct((bond, rows, bond), jnp.bfloat16)
+    dma = pltpu.SemaphoreType.DMA
+    return pl.pallas_call(
+        functools.partial(core_kernel, n, number),
+        out_shape=(slab, slab),
+        in_specs=[hbm, vmem, vmem, vmem],
+        out_specs=(vmem, vmem),
+        scratch_shapes=[
+            pltpu.VMEM((bond, bond, bond), jnp.bfloat16),
+            pltpu.VMEM((number, GROUP * 2 * rows, bond), jnp.bfloat16),
+            pltpu.VMEM((bond, rows, bond), jnp.bfloat16),
+            pltpu.VMEM((bond, rows, bond), jnp.bfloat16),
+            dma((steps,)),
+            dma((2, steps)),
+            dma((4, steps)),
+            dma((2, steps)),
+            dma((steps, n)),
+            dma((2, steps)),
+        ],
+        compiler_params=pltpu.CompilerParams(
+            collective_id=1, has_side_effects=True, vmem_limit_bytes=60 * 1024 * 1024
+        ),
+    )(upward, rc, coef, left_ops)
+
+
+def by_exchange(tensor, left_ops, right_ops, weights):
     bond = tensor.shape[1]
-    picks = term_ops[0]
-    weights = term_coef[0]
-    number = weights.shape[0]
-    left_ops = leg_ops[picks[:, 0]]
-    right_ops = leg_ops[picks[:, 1]]
     upward = lax.all_to_all(tensor, "shard", split_axis=2, concat_axis=0, tiled=True)
     regrouped = lax.all_to_all(tensor, "shard", split_axis=1, concat_axis=0, tiled=True)
     summed = jnp.zeros((bond, bond, upward.shape[2]), jnp.float32)
-    for term in range(number):
+    for term in range(weights.shape[0]):
         image = jnp.einsum(
             "lru,rs->lsu", upward, right_ops[term], preferred_element_type=jnp.float32
         ).astype(jnp.bfloat16)
@@ -129,10 +312,21 @@
     local = lax.all_to_all(
         summed.astype(jnp.bfloat16), "shard", split_axis=1, concat_axis=2, tiled=True
     )
-    env_part = jnp.einsum("lsu,lsv->uv", regrouped, local, preferred_element_type=jnp.float32)
+    return jnp.transpose(regrouped, (2, 1, 0)), jnp.transpose(local, (2, 1, 0))
+
+
+def shards(child_tensors, leg_ops, term_ops, term_coef, parent, top_env):
+    tensor = child_tensors[0]
+    picks = term_ops[0]
+    weights = term_coef[0]
+    left_ops = leg_ops[picks[:, 0]]
+    right_ops = leg_ops[picks[:, 1]]
+    form = local_of if lax.axis_size("shard") == 2 * LINE else by_exchange
+    slab, local = form(tensor, left_ops, right_ops, weights)
+    env_part = jnp.einsum("usl,vsl->uv", slab, local, preferred_element_type=jnp.float32)
     hole = hole_of(env_part, parent[0], top_env)
-    result = local.astype(jnp.float32) + jnp.einsum(
-        "lsu,uv->lsv", regrouped, hole, preferred_element_type=jnp.float32
+    result = jnp.transpose(local, (2, 1, 0)).astype(jnp.float32) + jnp.einsum(
+        "usl,uv->lsv", slab, hole, preferred_element_type=jnp.float32
     )
     return result.astype(jnp.bfloat16)[None]
 

time: 364 us -> 290 us (0.80)
  Pallas kernels: 31.1 us -> 241 us
  waiting for transfers between devices: 206 us -> 0 us
  matrix products: 61 us -> 18.5 us
  local copies, waits for them, and re-layouts: 48.7 us -> 20.7 us
  starting transfers between devices: 15.7 us -> 0 us
  other arithmetic: 0.01 us -> 8.73 us
    pallas_call x0 -> x1, Pallas kernels: none -> 216 us  [local_of(): pl.pallas_call(functools.partial(core_kernel, n, number), out_shape=(slab...]
    all_to_all x3 -> x0, waiting for transfers between devices: 206 us -> none  [the longest x1 87.6 us: shards(): lax.all_to_all(tensor, 'shard', split_axis=2, concat_axis=0, tiled=True)]
    dot_general x6 -> x2, matrix products: 61 us -> 18.5 us  [the longest x1 12.9 us: shards(): jnp.einsum('usl,vsl->uv', slab, local, preferred_element_type=jnp.float32)]
    all_to_all x3 -> x0, local copies, waits for them, and re-layouts: 16.3 us -> none  [the longest x1 6.76 us: shards(): lax.all_to_all(tensor, 'shard', split_axis=2, concat_axis=0, tiled=True)]
    all_to_all x3 -> x0, starting transfers between devices: 15.7 us -> none  [the longest x1 6.35 us: shards(): lax.all_to_all(tensor, 'shard', split_axis=2, concat_axis=0, tiled=True)]
    convert_element_type x1 -> x0, local copies, waits for them, and re-layouts: 7.83 us -> none  [shards(): summed.astype(jnp.bfloat16)]
    broadcast_in_dim x0 -> x1, other arithmetic: none -> 6.83 us  [shards(): return result.astype(jnp.bfloat16)[None]]
    squeeze x1 -> x0, local copies, waits for them, and re-layouts: 6.48 us -> none  [shards(): tensor = child_tensors[0]]
  transfers between devices with their start and end apart: 3 -> 0, of which waited for: 3 -> 0; matrix products, arithmetic and copies ran while one was open for 21% -> 0% of each run, Pallas kernels for 0% -> 0%
where the time goes in v3:
time: 290 us; the launch traced here: 289 us
  Pallas kernels  241 us (83%)
  local copies, waits for them, and re-layouts  20.7 us (7%)
  matrix products  18.5 us (6%)
  other arithmetic  8.73 us (3%)
    pallas_call x1, Pallas kernels, local_of(): pl.pallas_call(functools.partial(core_kernel, n, number), out_shape=(slab...  216 us
    pallas_call x1, Pallas kernels, hole_of(): pl.pallas_call(functools.partial(tail_kernel, n, nc, bond, factor), out_s...  25.4 us
    dot_general x1, matrix products, shards(): jnp.einsum('usl,vsl->uv', slab, local, preferred_element_type=jnp.float32)  12.9 us
    broadcast_in_dim x1, local copies, waits for them, and re-layouts, shards(): return result.astype(jnp.bfloat16)[None]  8.49 us
    unnamed x5, local copies, waits for them, and re-layouts  7.84 us
    broadcast_in_dim x1, other arithmetic, shards(): return result.astype(jnp.bfloat16)[None]  6.83 us

profile of v3, /device:TPU:0, one launch (start us, length us, event | category | flops | bytes accessed | tf_op | source)
XLA Modules:
  0.0 289.0 jit_solution(8991627863019487159)
XLA Ops:
  0.0 0.0 copy-start
  0.0 0.8 pad_maximum_fusion.1
  0.8 0.1 fusion.20
  0.9 0.1 add_multiply_fusion
  1.0 0.1 iota_add_fusion
  1.0 0.8 fusion.21
  1.8 0.1 broadcast_in_dim.4
  1.9 0.1 fusion.18
  2.0 0.8 broadcast_in_dim_reshape.4.coef_ref
  2.8 0.0 copy-done
  2.8 1.4 gather_fusion.2
  4.2 0.6 gather_fusion
  4.8 0.2 copy.24
  5.0 0.6 gather_fusion.1
  5.6 0.7 copy.25
  6.3 7.8 %copy.23 = bf16[1,32,256,256]{2,1,3,0:T(8,128)(2,1)} copy(bf16[1,32,256,256]{3,2,1,0:T(8,128)(2,1)} %param.6) | data formatting | bytes 8388608 | tf_op args[0]
  14.1 215.7 %shard_map.64 = (bf16[256,32,256]{2,1,0:T(8,128)(2,1)}, bf16[256,32,256]{2,1,0:T(8,128)(2,1)}) custom-call(bf16[256,32,256]{2,1,0:T(8,128)(2,1)} %bitcast.33, bf16[320,256]{1,0:T(8,128)(2,1)} %bitcast.36, f32[320,1]{1,0:T(8,128)} %broadcast_in_dim_reshape.4.coef_ref, bf16[4,256,256]{2,1,0:T(8,128)(2,1)} %gather_fusion.2), custom_call_target="tpu_custom_call" | custom-call | tf_op jit(solution)/shard_map/pallas_call | solution.py:277
  229.8 12.9 %fusion.12 = bf16[256,256]{1,0:T(8,128)(2,1)} fusion(bf16[256,32,256]{2,1,0:T(8,128)(2,1)} %get-tuple-element.7, bf16[256,32,256]{2,1,0:T(8,128)(2,1)} %get-tuple-element.8), kind=kOutput, calls=%fused_computation.12 | convolution fusion | flops 1073807360 | bytes 8519680 | tf_op jit(solution)/shard_map/usl,vsl->uv/dot_general | solution.py:326
  242.7 25.4 %shard_map.65 = bf16[256,256]{1,0:T(8,128)(2,1)} custom-call(bf16[8,32,256]{2,1,0:T(8,128)(2,1)} %bitcast.39, bf16[32,256]{1,0:T(8,128)(2,1)} %bitcast.40, f32[8,32,256]{2,1,0:T(8,128)} %bitcast.38), custom_call_target="tpu_custom_call" | custom-call | tf_op jit(solution)/shard_map/pallas_call | solution.py:92
  268.1 0.0 copy-start.1
  268.1 5.6 %fusion.4 = f32[256,32,256]{2,0,1:T(8,128)S(1)} fusion(bf16[256,32,256]{2,1,0:T(8,128)(2,1)} %get-tuple-element.8, bf16[256,256]{1,0:T(8,128)(2,1)} %shard_map.65), kind=kOutput, calls=%fused_computation.8 | convolution fusion | flops 1073741824 | bytes 12713984 | tf_op jit(solution)/shard_map/usl,uv->lsv/dot_general | solution.py:328
  273.7 0.0 copy-done.1
  273.7 6.8 %fusion.1 = bf16[1,256,32,256]{1,2,3,0:T(8,128)(2,1)} fusion(f32[256,32,256]{2,0,1:T(8,128)S(1)} %fusion.4, bf16[256,32,256]{2,1,0:T(8,128)(2,1)S(1)} %copy-done.1), kind=kLoop, calls=%fused_computation.5 | loop fusion | flops 6291456 | bytes 16777216 | tf_op jit(solution)/shard_map/broadcast_in_dim | solution.py:331
  280.5 8.5 %copy.32 = bf16[1,256,32,256]{3,2,1,0:T(8,128)(2,1)} copy(bf16[1,256,32,256]{1,2,3,0:T(8,128)(2,1)} %fusion.1) | data formatting | bytes 8388608 | tf_op jit(solution)/shard_map/broadcast_in_dim | solution.py:331
  (3 shorter events, 0.0 us)
Async XLA Ops:
  0.0 2.8 copy-start
  268.1 5.6 %copy-start.1 = (bf16[256,32,256]{2,1,0:T(8,128)(2,1)S(1)}, bf16[256,32,256]{2,1,0:T(8,128)(2,1)}, u32[]{:S(2)}) copy-start(bf16[256,32,256]{2,1,0:T(8,128)(2,1)} %get-tuple-element.7) | copy-start | bytes 12582916

commit v4 on v3

--- a/solution.py
+++ b/solution.py
@@ -108,8 +108,9 @@
     )(env_part.astype(jnp.bfloat16).reshape(n, rows, bond), parent_block, top_env.reshape(n, rows, width))
 
 
-CHUNK = 16
+CHUNK = 8
 GROUP = 8
+AHEAD = 3
 LINE = 4
 
 
@@ -197,13 +198,12 @@
             pass_on(q, mate, csem.at[1, q], across).start()
             pass_on(q, mate, fsem.at[1, q], twin).start()
 
-        relay(0)
-        relay(1)
+        loop(AHEAD, relay)
 
         def chunk(q):
-            @pl.when(q + 2 < steps)
+            @pl.when(q + AHEAD < steps)
             def _():
-                relay(q + 2)
+                relay(q + AHEAD)
 
             for slot, j in ((2, across), (3, far)):
                 pass_on(q, j, fsem.at[slot, q], twin).wait_recv()
@@ -325,10 +325,10 @@
     slab, local = form(tensor, left_ops, right_ops, weights)
     env_part = jnp.einsum("usl,vsl->uv", slab, local, preferred_element_type=jnp.float32)
     hole = hole_of(env_part, parent[0], top_env)
-    result = jnp.transpose(local, (2, 1, 0)).astype(jnp.float32) + jnp.einsum(
-        "usl,uv->lsv", slab, hole, preferred_element_type=jnp.float32
-    )
-    return result.astype(jnp.bfloat16)[None]
+    result = local.astype(jnp.float32) + jnp.einsum(
+        "uv,usl->vsl", hole, slab, preferred_element_type=jnp.float32
+    )
+    return jnp.transpose(result.astype(jnp.bfloat16), (2, 1, 0))[None]
 
 
 def solution(mesh):

time: 290 us -> 285 us (0.983)
  Pallas kernels: 241 us -> 237 us
    pallas_call x1, Pallas kernels: 216 us -> 211 us  [local_of(): pl.pallas_call(functools.partial(core_kernel, n, number), out_shape=(slab...]
where the time goes in v4:
time: 285 us
  Pallas kernels  237 us (83%)
  local copies, waits for them, and re-layouts  20.7 us (7%)
  matrix products  18.3 us (6%)
  other arithmetic  8.73 us (3%)
    pallas_call x1, Pallas kernels, local_of(): pl.pallas_call(functools.partial(core_kernel, n, number), out_shape=(slab...  211 us
    pallas_call x1, Pallas kernels, hole_of(): pl.pallas_call(functools.partial(tail_kernel, n, nc, bond, factor), out_s...  25.5 us
    dot_general x1, matrix products, shards(): jnp.einsum('usl,vsl->uv', slab, local, preferred_element_type=jnp.float32)  12.9 us
    broadcast_in_dim x1, local copies, waits for them, and re-layouts, shards(): return jnp.transpose(result.astype(jnp.bfloat16), (2, 1, 0))[None]  8.49 us
    unnamed x5, local copies, waits for them, and re-layouts  7.84 us
    broadcast_in_dim x1, other arithmetic, shards(): return jnp.transpose(result.astype(jnp.bfloat16), (2, 1, 0))[None]  6.83 us

profile of v4, /device:TPU:0, one launch (start us, length us, event | category | flops | bytes accessed | tf_op | source)
XLA Modules:
  0.0 284.7 jit_solution(5778042738355004324)
XLA Ops:
  0.0 0.0 copy-start
  0.0 0.8 pad_maximum_fusion.1
  0.8 0.1 fusion.20
  0.9 0.1 add_multiply_fusion
  1.0 0.1 iota_add_fusion
  1.0 0.8 fusion.21
  1.8 0.1 broadcast_in_dim.4
  1.9 0.1 fusion.18
  2.0 0.8 broadcast_in_dim_reshape.4.coef_ref
  2.8 0.0 copy-done
  2.8 1.4 gather_fusion.2
  4.2 0.6 gather_fusion
  4.8 0.2 copy.24
  5.0 0.6 gather_fusion.1
  5.6 0.7 copy.25
  6.3 7.8 %copy.23 = bf16[1,32,256,256]{2,1,3,0:T(8,128)(2,1)} copy(bf16[1,32,256,256]{3,2,1,0:T(8,128)(2,1)} %param.6) | data formatting | bytes 8388608 | tf_op args[0]
  14.1 211.4 %shard_map.64 = (bf16[256,32,256]{2,1,0:T(8,128)(2,1)}, bf16[256,32,256]{2,1,0:T(8,128)(2,1)}) custom-call(bf16[256,32,256]{2,1,0:T(8,128)(2,1)} %bitcast.33, bf16[320,256]{1,0:T(8,128)(2,1)} %bitcast.36, f32[320,1]{1,0:T(8,128)} %broadcast_in_dim_reshape.4.coef_ref, bf16[4,256,256]{2,1,0:T(8,128)(2,1)} %gather_fusion.2), custom_call_target="tpu_custom_call" | custom-call | tf_op jit(solution)/shard_map/pallas_call | solution.py:277
  225.5 12.9 %fusion.12 = bf16[256,256]{1,0:T(8,128)(2,1)} fusion(bf16[256,32,256]{2,1,0:T(8,128)(2,1)} %get-tuple-element.7, bf16[256,32,256]{2,1,0:T(8,128)(2,1)} %get-tuple-element.8), kind=kOutput, calls=%fused_computation.12 | convolution fusion | flops 1073807360 | bytes 8519680 | tf_op jit(solution)/shard_map/usl,vsl->uv/dot_general | solution.py:326
  238.4 25.5 %shard_map.65 = bf16[256,256]{1,0:T(8,128)(2,1)} custom-call(bf16[8,32,256]{2,1,0:T(8,128)(2,1)} %bitcast.39, bf16[32,256]{1,0:T(8,128)(2,1)} %bitcast.40, f32[8,32,256]{2,1,0:T(8,128)} %bitcast.38), custom_call_target="tpu_custom_call" | custom-call | tf_op jit(solution)/shard_map/pallas_call | solution.py:92
  263.9 0.0 copy-start.1
  263.9 5.5 %fusion.4 = f32[256,32,256]{2,0,1:T(8,128)S(1)} fusion(bf16[256,32,256]{2,1,0:T(8,128)(2,1)} %get-tuple-element.8, bf16[256,256]{1,0:T(8,128)(2,1)} %shard_map.65), kind=kOutput, calls=%fused_computation.8 | convolution fusion | flops 1073741824 | bytes 12713984 | tf_op jit(solution)/shard_map/uv,usl->vsl/dot_general | solution.py:328
  269.4 0.0 copy-done.1
  269.4 6.8 %fusion.1 = bf16[1,256,32,256]{1,2,3,0:T(8,128)(2,1)} fusion(f32[256,32,256]{2,0,1:T(8,128)S(1)} %fusion.4, bf16[256,32,256]{2,1,0:T(8,128)(2,1)S(1)} %copy-done.1), kind=kLoop, calls=%fused_computation.5 | loop fusion | flops 6291456 | bytes 16777216 | tf_op jit(solution)/shard_map/broadcast_in_dim | solution.py:331
  276.2 8.5 %copy.32 = bf16[1,256,32,256]{3,2,1,0:T(8,128)(2,1)} copy(bf16[1,256,32,256]{1,2,3,0:T(8,128)(2,1)} %fusion.1) | data formatting | bytes 8388608 | tf_op jit(solution)/shard_map/broadcast_in_dim | solution.py:331
  (3 shorter events, 0.0 us)
Async XLA Ops:
  0.0 2.8 copy-start
  263.9 5.5 %copy-start.1 = (bf16[256,32,256]{2,1,0:T(8,128)(2,1)S(1)}, bf16[256,32,256]{2,1,0:T(8,128)(2,1)}, u32[]{:S(2)}) copy-start(bf16[256,32,256]{2,1,0:T(8,128)(2,1)} %get-tuple-element.7) | copy-start | bytes 12582916
